TPU v7x, 32 devices: a whole 2x2x4 slice. The times are simulated.
32 devices in a mesh: member: 2 (over y), domain: 4 (over z), role: 4 (over x, core).
Axes of the slice: x: 2, y: 2, z: 4, core: 2. Of those that a mesh axis runs over, the one named last changes fastest.
Arguments:
- ensemble: float32 [256, 32, 512], P('member', 'domain', 'role'), may hold values from -6 to 6
- diffusion: float32 [32, 512], P('domain', 'role'), may hold values from 0.02 to 0.1
- drift_rows: float32 [32, 512], P('domain', 'role'), may hold values from 0.05 to 0.3
- drift_cols: float32 [32, 512], P('domain', 'role'), may hold values from 0.05 to 0.3
- observed_cells: int32 [4, 1024], P('domain'), may hold values from 0 to 4095
- observed_count: int32 [4], P('domain'), may hold values from 256 to 1024
- observed_values: float32 [4, 1024], P('domain'), may hold values from -6 to 6
- observed_weights: float32 [4, 1024], P('domain'), may hold values from 0.5 to 4
Outputs:
- analysis: float32 [256, 32, 512], P('member', 'domain', 'role')
All inputs are finite; a program needn't handle non-finite values.
Results may differ from a plain program's by a relative error of at most 0.0003.
Values sent between devices are 32-bit elements; how exact they have to be, the bound alone decides.
No kernel may reach another device: no remote copies, remote signals or barrier semaphores. Data moves between devices by JAX's collectives and lax.ppermute only.
A program may use at most 64 MiB of HBM per device.

v0:
```python
import jax
import jax.numpy as jnp
from jax import lax
from jax.sharding import PartitionSpec as P

STEPS = 4
ITERS = 6
precise = lax.Precision.HIGHEST


def extended(value, sides, width):
    for axis, dim in sides:
        size, length = (lax.axis_size(axis), value.shape[dim])
        up = [(i, (i + 1) % size) for i in range(size)]
        down = [(j, i) for i, j in up]
        last = lax.slice_in_dim(value, length - width, length, axis=dim)
        initial = lax.slice_in_dim(value, 0, width, axis=dim)
        before = lax.ppermute(last, axis, up)
        after = lax.ppermute(initial, axis, down)
        value = jnp.concatenate([before, value, after], axis=dim)
    return value


def inverse_root(matrix):
    extent = matrix.shape[0]
    identity = jnp.eye(extent, dtype=jnp.float32)
    scaling = jnp.sqrt(jnp.sum(matrix * matrix))
    current = matrix / scaling
    inverse = identity
    for repeat in range(ITERS):
        middle = 0.5 * (3.0 * identity - jnp.dot(inverse, current, precision=precise))
        current = jnp.dot(current, middle, precision=precise)
        inverse = jnp.dot(middle, inverse, precision=precise)
    return (inverse, scaling)


def analysis_weights(gram_sum, innovation):
    extent = gram_sum.shape[0]
    matrix = gram_sum + (extent - 1.0) * jnp.eye(extent, dtype=jnp.float32)
    inverse, scaling = inverse_root(matrix)
    spread = jnp.sqrt((extent - 1.0) / scaling) * inverse
    shifted = (
        jnp.dot(inverse, jnp.dot(inverse, innovation, precision=precise), precision=precise)
        / scaling
    )
    return spread + shifted[:, None]


def shards(
    ensemble,
    diffusion,
    drift_rows,
    drift_cols,
    observed_cells,
    observed_count,
    observed_values,
    observed_weights,
):
    current = ensemble
    for repeat in range(STEPS):
        padded = extended(current, (("domain", 1), ("role", 2)), 1)
        inner = padded[:, 1:-1, 1:-1]
        ahead_rows = padded[:, 2:, 1:-1]
        behind_rows = padded[:, :-2, 1:-1]
        ahead_cols = padded[:, 1:-1, 2:]
        behind_cols = padded[:, 1:-1, :-2]
        spread = ahead_rows + behind_rows + ahead_cols + behind_cols - 4.0 * inner
        current = (
            inner
            + diffusion * spread
            - drift_rows * (inner - behind_rows)
            - drift_cols * (inner - behind_cols)
        )
    member_groups = lax.axis_size("member")
    role_groups = lax.axis_size("role")
    local_members, rows_local, cols_local = current.shape
    members_all = local_members * member_groups
    own_rows = rows_local // (member_groups * role_groups)
    full_cols = cols_local * role_groups
    position = lax.axis_index("member") * role_groups + lax.axis_index("role")
    cell_index = observed_cells[0]
    counts = observed_count[0]
    values = observed_values[0]
    weights = observed_weights[0]
    row_of = cell_index // full_cols
    col_of = cell_index % full_cols
    owned = row_of // own_rows == position
    usable = owned & (jnp.arange(cell_index.shape[0]) < counts)
    row_local = jnp.where(owned, row_of - position * own_rows, 0)
    received = lax.all_to_all(current, ("member", "role"), split_axis=1, concat_axis=0, tiled=True)
    blocks = received.reshape(member_groups, role_groups, local_members, own_rows, cols_local)
    picked = blocks[:, col_of // cols_local, :, row_local, col_of % cols_local]
    observed = picked.reshape(-1, members_all).T
    centre_obs = jnp.mean(observed, axis=0)
    deviation = observed - centre_obs
    weighted = deviation * jnp.where(usable, weights, jnp.float32(0.0))
    gram_sum, innovation = lax.psum(
        (
            jnp.dot(weighted, deviation.T, precision=precise),
            jnp.dot(weighted, values - centre_obs, precision=precise),
        ),
        ("member", "role"),
    )
    mixing = analysis_weights(gram_sum, innovation)
    flat_blocks = blocks.reshape(member_groups, role_groups, local_members, own_rows * cols_local)
    centre = jnp.sum(flat_blocks, axis=(0, 2)) / members_all
    deviation_field = flat_blocks - centre[None, :, None, :]
    mixing_blocks = mixing.reshape(member_groups, local_members, member_groups, local_members)
    updated = jnp.einsum("mrkc,mknj->nrjc", deviation_field, mixing_blocks, precision=precise)
    updated = updated + centre[None, :, None, :]
    returned = lax.all_to_all(
        updated.reshape(-1, own_rows, cols_local),
        ("member", "role"),
        split_axis=0,
        concat_axis=1,
        tiled=True,
    )
    return returned


def solution(mesh):
    placed = (
        P("member", "domain", "role"),
        P("domain", "role"),
        P("domain", "role"),
        P("domain", "role"),
        P("domain", None),
        P("domain"),
        P("domain", None),
        P("domain", None),
    )
    return jax.shard_map(
        shards, mesh=mesh, in_specs=placed, out_specs=P("member", "domain", "role"), check_vma=False
    )
```

profile of v0, /device:TPU:0, one launch (start us, length us, event | category | flops | bytes accessed | tf_op | source)
XLA Modules:
  0.0 175.5 jit_solution(9322372956486564252)
XLA Ops:
  6.5 1.2 copy.67
  7.8 3.1 %collective-permute-start.1 = (f32[128,1,128]{2,0,1:T(8,128)S(1)}, f32[128,1,128]{2,0,1:T(8,128)S(1)}, u32[]{:S(2)}, u32[]{:S(2)}) collective-permute-start(f32[128,1,128]{2,0,1:T(8,128)S(1)} %get-tuple-element.20), channel_id=1, source_target_pairs={{0,4},{4,8},{8,12},{12,0},{1,5},{5,9},{9,13},{13,1},{2,6},{6,10},{... | collective-permute-start | bytes 196616 | tf_op jit(solution)/shard_map/ppermute | solution.py:18
  10.9 2.1 %collective-permute-start = (f32[128,1,128]{2,0,1:T(8,128)S(1)}, f32[128,1,128]{2,0,1:T(8,128)S(1)}, u32[]{:S(2)}, u32[]{:S(2)}) collective-permute-start(f32[128,1,128]{2,0,1:T(8,128)S(1)} %get-tuple-element.19), channel_id=1, source_target_pairs={{4,0},{8,4},{12,8},{0,12},{5,1},{9,5},{13,9},{1,13},{6,2},{10,6},{... | collective-permute-start | bytes 196616 | tf_op jit(solution)/shard_map/ppermute | solution.py:19
  13.0 2.3 %collective-permute-done.1 = f32[128,1,128]{2,0,1:T(8,128)S(1)} collective-permute-done((f32[128,1,128]{2,0,1:T(8,128)S(1)}, f32[128,1,128]{2,0,1:T(8,128)S(1)}, u32[]{:S(2)}, u32[]{:S(2)}) %collective-permute-start.1) | collective-permute-done | bytes 65568 | tf_op jit(solution)/shard_map/ppermute | solution.py:18
  15.3 0.5 collective-permute-done
  16.6 0.5 collective-permute-start.3
  17.1 0.6 collective-permute-done.2
  18.0 1.7 collective-permute-done.3
  19.9 0.5 fusion.46
  20.4 3.2 %collective-permute-start.4 = (f32[128,1,128]{2,0,1:T(8,128)S(1)}, f32[128,1,128]{2,0,1:T(8,128)S(1)}, u32[]{:S(2)}, u32[]{:S(2)}) collective-permute-start(f32[128,1,128]{2,0,1:T(8,128)S(1)} %get-tuple-element.18), channel_id=1, source_target_pairs={{4,0},{8,4},{12,8},{0,12},{5,1},{9,5},{13,9},{1,13},{6,2},{10,6},{... | collective-permute-start | bytes 196616 | tf_op jit(solution)/shard_map/ppermute | solution.py:19
  23.7 2.5 %collective-permute-done.4 = f32[128,1,128]{2,0,1:T(8,128)S(1)} collective-permute-done((f32[128,1,128]{2,0,1:T(8,128)S(1)}, f32[128,1,128]{2,0,1:T(8,128)S(1)}, u32[]{:S(2)}, u32[]{:S(2)}) %collective-permute-start.4) | collective-permute-done | bytes 65568 | tf_op jit(solution)/shard_map/ppermute | solution.py:19
  26.2 3.6 %collective-permute-done.5 = f32[128,1,128]{2,0,1:T(8,128)S(1)} collective-permute-done((f32[128,1,128]{2,0,1:T(8,128)S(1)}, f32[128,1,128]{2,0,1:T(8,128)S(1)}, u32[]{:S(2)}, u32[]{:S(2)}) %collective-permute-start.5) | collective-permute-done | bytes 65568 | tf_op jit(solution)/shard_map/ppermute | solution.py:18
  30.5 0.5 collective-permute-start.7
  31.1 0.6 collective-permute-done.6
  31.9 1.7 collective-permute-done.7
  33.9 0.5 fusion.36
  34.4 0.8 collective-permute-start.8
  35.1 1.3 collective-permute-start.9
  36.5 2.2 %collective-permute-done.8 = f32[128,1,128]{2,0,1:T(8,128)S(1)} collective-permute-done((f32[128,1,128]{2,0,1:T(8,128)S(1)}, f32[128,1,128]{2,0,1:T(8,128)S(1)}, u32[]{:S(2)}, u32[]{:S(2)}) %collective-permute-start.8) | collective-permute-done | bytes 65568 | tf_op jit(solution)/shard_map/ppermute | solution.py:19
  38.7 2.5 %collective-permute-done.9 = f32[128,1,128]{2,0,1:T(8,128)S(1)} collective-permute-done((f32[128,1,128]{2,0,1:T(8,128)S(1)}, f32[128,1,128]{2,0,1:T(8,128)S(1)}, u32[]{:S(2)}, u32[]{:S(2)}) %collective-permute-start.9) | collective-permute-done | bytes 65568 | tf_op jit(solution)/shard_map/ppermute | solution.py:18
  42.0 0.5 collective-permute-start.11
  42.5 0.6 collective-permute-done.10
  43.4 1.7 collective-permute-done.11
  45.3 0.5 fusion.26
  45.8 0.7 collective-permute-start.12
  46.5 1.4 collective-permute-start.13
  47.9 2.9 %collective-permute-done.12 = f32[128,1,128]{2,0,1:T(8,128)S(1)} collective-permute-done((f32[128,1,128]{2,0,1:T(8,128)S(1)}, f32[128,1,128]{2,0,1:T(8,128)S(1)}, u32[]{:S(2)}, u32[]{:S(2)}) %collective-permute-start.12) | collective-permute-done | bytes 65568 | tf_op jit(solution)/shard_map/ppermute | solution.py:19
  50.9 1.7 collective-permute-done.13
  53.3 0.5 collective-permute-start.15
  53.8 0.6 collective-permute-done.14
  54.7 1.7 collective-permute-done.15
  56.7 1.3 fusion.16
  57.9 3.5 %all-to-all-start = ((f32[128,8,128]{2,0,1:T(8,128)}), f32[128,8,128]{2,0,1:T(8,128)S(1)}, u32[]{:S(2)}, u32[]{:S(2)}) async-start(f32[128,8,128]{2,0,1:T(8,128)} %fusion.16), calls=%async_computation | async-start | bytes 1048576 | tf_op jit(solution)/shard_map/all_to_all | solution.py:90
  62.5 0.6 copy-done.6
  63.1 8.0 %all-to-all-done = f32[128,8,128]{2,0,1:T(8,128)S(1)} async-done(((f32[128,8,128]{2,0,1:T(8,128)}), f32[128,8,128]{2,0,1:T(8,128)S(1)}, u32[]{:S(2)}, u32[]{:S(2)}) %all-to-all-start) | async-done | bytes 524320 | tf_op jit(solution)/shard_map/all_to_all | solution.py:90
  71.4 4.5 %gather_fusion = f32[1024,2,128]{2,1,0:T(2,128)S(1)} fusion(f32[2,4,128,1,128]{2,0,4,3,1:T(2,128)S(1)} %copy.82, s32[1024]{0:T(1024)S(1)} %bitcast.100), kind=kCustom, calls=%fused_computation | custom fusion | bytes 2109440 | tf_op jit(solution)/shard_map/gather | solution.py:92
  75.8 1.8 %reduce_sum.34 = f32[1024]{0:T(1024)S(1)} reduce(f32[1024,2,128]{2,1,0:T(2,128)S(1)} %gather_fusion, f32[]{:T(128)} %constant.90.clone.1), dimensions={1,2}, to_apply=%region_0.1 | reduce | flops 261120 | bytes 1052676 | tf_op jit(solution)/shard_map/reduce_sum | solution.py:94
  77.7 3.0 %fusion = f32[256,256]{1,0:T(8,128)} fusion(f32[128,8,2,128]{3,2,1,0:T(2,128)S(1)} %bitcast.101, f32[1024]{0:T(1024)S(1)} %bitcast.108, f32[1024]{0:T(1024)S(1)} %get-tuple-element.22), kind=kOutput, calls=%fused_computation.2 | convolution fusion | flops 806092800 | bytes 1318912 | tf_op jit(solution)/shard_map/dot_general | solution.py:99
  80.6 0.8 fusion.9
  81.4 12.0 %psum.15 = f32[256]{0:T(256)S(1)} all-reduce(f32[256]{0:T(256)S(1)} %bitcast.113), channel_id=1, replica_groups=mesh['member'=2,'domain'=4,'role'=4] {'member','role'}, use_global_device_ids=true, to_apply=%region_3.4 | all-reduce | flops 256 | bytes 2048 | tf_op jit(solution)/shard_map/psum | solution.py:97
  93.5 51.4 %all-reduce.2.cloned.1.call-done = f32[256,256]{1,0:T(8,128)} async-done(((f32[256,256]{1,0:T(8,128)}), f32[256,256]{1,0:T(8,128)}) %all-reduce.2.cloned.1.call-update) | async-done | bytes 262160 | tf_op jit(solution)/shard_map/psum | solution.py:97
  144.9 1.7 multiply_reduce_fusion
  147.9 0.4 fusion.59
  149.5 0.4 fusion.6
  150.6 0.4 fusion.5
  154.7 0.6 fusion.2
  155.4 12.1 %all_to_all.33 = f32[1024,1,128]{2,1,0:T(1,128)S(1)} all-to-all(f32[1024,1,128]{2,1,0:T(1,128)S(1)} %bitcast.105), channel_id=1, replica_groups=mesh['member'=2,'domain'=4,'role'=4] {'member','role'}, dimensions={0} | all-to-all | bytes 1048576 | tf_op jit(solution)/shard_map/all_to_all | solution.py:111
  167.5 1.1 copy.86
  (78 shorter events, 11.9 us)
Async XLA Ops:
  6.5 8.7 %copy-start = (f32[128,8,128]{2,1,0:T(8,128)S(1)}, f32[128,8,128]{2,1,0:T(8,128)}, u32[]{:S(2)}) copy-start(f32[128,8,128]{2,1,0:T(8,128)} %param.8) | copy-start | bytes 1572868
  7.8 7.5 %collective-permute-start.1 = (f32[128,1,128]{2,0,1:T(8,128)S(1)}, f32[128,1,128]{2,0,1:T(8,128)S(1)}, u32[]{:S(2)}, u32[]{:S(2)}) collective-permute-start(f32[128,1,128]{2,0,1:T(8,128)S(1)} %get-tuple-element.20), channel_id=1, source_target_pairs={{0,4},{4,8},{8,12},{12,0},{1,5},{5,9},{9,13},{13,1},{2,6},{6,10},{... | collective-permute-start | bytes 196616 | tf_op jit(solution)/shard_map/ppermute | solution.py:18
  10.9 5.0 %collective-permute-start = (f32[128,1,128]{2,0,1:T(8,128)S(1)}, f32[128,1,128]{2,0,1:T(8,128)S(1)}, u32[]{:S(2)}, u32[]{:S(2)}) collective-permute-start(f32[128,1,128]{2,0,1:T(8,128)S(1)} %get-tuple-element.19), channel_id=1, source_target_pairs={{4,0},{8,4},{12,8},{0,12},{5,1},{9,5},{13,9},{1,13},{6,2},{10,6},{... | collective-permute-start | bytes 196616 | tf_op jit(solution)/shard_map/ppermute | solution.py:19
  16.3 1.4 collective-permute-start.2
  16.6 3.1 %collective-permute-start.3 = (f32[128,10,1]{0,2,1:T(1,128)S(1)}, f32[128,10,1]{0,2,1:T(1,128)S(1)}, u32[]{:S(2)}, u32[]{:S(2)}) collective-permute-start(f32[128,10,1]{0,2,1:T(1,128)S(1)} %copy.64), channel_id=1, source_target_pairs={{0,1},{1,2},{2,3},{3,0},{4,5},{5,6},{6,7},{7,4},{8,9},{9,10},{10,1... | collective-permute-start | bytes 15368 | tf_op jit(solution)/shard_map/ppermute | solution.py:18
  17.9 2.0 %copy-start.2 = (f32[8,128]{1,0:T(8,128)S(1)}, f32[8,128]{1,0:T(8,128)}, u32[]{:S(2)}) copy-start(f32[8,128]{1,0:T(8,128)} %param.11) | copy-start | bytes 12292
  18.0 2.0 %copy-start.3 = (f32[8,128]{1,0:T(8,128)S(1)}, f32[8,128]{1,0:T(8,128)}, u32[]{:S(2)}) copy-start(f32[8,128]{1,0:T(8,128)} %param.10) | copy-start | bytes 12292
  18.0 2.0 %copy-start.4 = (f32[8,128]{1,0:T(8,128)S(1)}, f32[8,128]{1,0:T(8,128)}, u32[]{:S(2)}) copy-start(f32[8,128]{1,0:T(8,128)} %param.9) | copy-start | bytes 12292
  20.4 5.7 %collective-permute-start.4 = (f32[128,1,128]{2,0,1:T(8,128)S(1)}, f32[128,1,128]{2,0,1:T(8,128)S(1)}, u32[]{:S(2)}, u32[]{:S(2)}) collective-permute-start(f32[128,1,128]{2,0,1:T(8,128)S(1)} %get-tuple-element.18), channel_id=1, source_target_pairs={{4,0},{8,4},{12,8},{0,12},{5,1},{9,5},{13,9},{1,13},{6,2},{10,6},{... | collective-permute-start | bytes 196616 | tf_op jit(solution)/shard_map/ppermute | solution.py:19
  23.7 6.1 %collective-permute-start.5 = (f32[128,1,128]{2,0,1:T(8,128)S(1)}, f32[128,1,128]{2,0,1:T(8,128)S(1)}, u32[]{:S(2)}, u32[]{:S(2)}) collective-permute-start(f32[128,1,128]{2,0,1:T(8,128)S(1)} %get-tuple-element.17), channel_id=1, source_target_pairs={{0,4},{4,8},{8,12},{12,0},{1,5},{5,9},{9,13},{13,1},{2,6},{6,10},{... | collective-permute-start | bytes 196616 | tf_op jit(solution)/shard_map/ppermute | solution.py:18
  30.3 1.4 collective-permute-start.6
  30.5 3.1 %collective-permute-start.7 = (f32[128,10,1]{0,2,1:T(1,128)S(1)}, f32[128,10,1]{0,2,1:T(1,128)S(1)}, u32[]{:S(2)}, u32[]{:S(2)}) collective-permute-start(f32[128,10,1]{0,2,1:T(1,128)S(1)} %copy.72), channel_id=1, source_target_pairs={{0,1},{1,2},{2,3},{3,0},{4,5},{5,6},{6,7},{7,4},{8,9},{9,10},{10,1... | collective-permute-start | bytes 15368 | tf_op jit(solution)/shard_map/ppermute | solution.py:18
  34.4 4.3 %collective-permute-start.8 = (f32[128,1,128]{2,0,1:T(8,128)S(1)}, f32[128,1,128]{2,0,1:T(8,128)S(1)}, u32[]{:S(2)}, u32[]{:S(2)}) collective-permute-start(f32[128,1,128]{2,0,1:T(8,128)S(1)} %get-tuple-element.16), channel_id=1, source_target_pairs={{4,0},{8,4},{12,8},{0,12},{5,1},{9,5},{13,9},{1,13},{6,2},{10,6},{... | collective-permute-start | bytes 196616 | tf_op jit(solution)/shard_map/ppermute | solution.py:19
  35.1 6.1 %collective-permute-start.9 = (f32[128,1,128]{2,0,1:T(8,128)S(1)}, f32[128,1,128]{2,0,1:T(8,128)S(1)}, u32[]{:S(2)}, u32[]{:S(2)}) collective-permute-start(f32[128,1,128]{2,0,1:T(8,128)S(1)} %get-tuple-element.15), channel_id=1, source_target_pairs={{0,4},{4,8},{8,12},{12,0},{1,5},{5,9},{9,13},{13,1},{2,6},{6,10},{... | collective-permute-start | bytes 196616 | tf_op jit(solution)/shard_map/ppermute | solution.py:18
  41.7 1.4 collective-permute-start.10
  42.0 3.1 %collective-permute-start.11 = (f32[128,10,1]{0,2,1:T(1,128)S(1)}, f32[128,10,1]{0,2,1:T(1,128)S(1)}, u32[]{:S(2)}, u32[]{:S(2)}) collective-permute-start(f32[128,10,1]{0,2,1:T(1,128)S(1)} %copy.76), channel_id=1, source_target_pairs={{0,1},{1,2},{2,3},{3,0},{4,5},{5,6},{6,7},{7,4},{8,9},{9,10},{10,1... | collective-permute-start | bytes 15368 | tf_op jit(solution)/shard_map/ppermute | solution.py:18
  45.8 5.0 %collective-permute-start.12 = (f32[128,1,128]{2,0,1:T(8,128)S(1)}, f32[128,1,128]{2,0,1:T(8,128)S(1)}, u32[]{:S(2)}, u32[]{:S(2)}) collective-permute-start(f32[128,1,128]{2,0,1:T(8,128)S(1)} %get-tuple-element.14), channel_id=1, source_target_pairs={{4,0},{8,4},{12,8},{0,12},{5,1},{9,5},{13,9},{1,13},{6,2},{10,6},{... | collective-permute-start | bytes 196616 | tf_op jit(solution)/shard_map/ppermute | solution.py:19
  46.5 6.1 %collective-permute-start.13 = (f32[128,1,128]{2,0,1:T(8,128)S(1)}, f32[128,1,128]{2,0,1:T(8,128)S(1)}, u32[]{:S(2)}, u32[]{:S(2)}) collective-permute-start(f32[128,1,128]{2,0,1:T(8,128)S(1)} %get-tuple-element.13), channel_id=1, source_target_pairs={{0,4},{4,8},{8,12},{12,0},{1,5},{5,9},{9,13},{13,1},{2,6},{6,10},{... | collective-permute-start | bytes 196616 | tf_op jit(solution)/shard_map/ppermute | solution.py:18
  53.1 1.4 collective-permute-start.14
  53.3 3.1 %collective-permute-start.15 = (f32[128,10,1]{0,2,1:T(1,128)S(1)}, f32[128,10,1]{0,2,1:T(1,128)S(1)}, u32[]{:S(2)}, u32[]{:S(2)}) collective-permute-start(f32[128,10,1]{0,2,1:T(1,128)S(1)} %copy.80), channel_id=1, source_target_pairs={{0,1},{1,2},{2,3},{3,0},{4,5},{5,6},{6,7},{7,4},{8,9},{9,10},{10,1... | collective-permute-start | bytes 15368 | tf_op jit(solution)/shard_map/ppermute | solution.py:18
  57.9 13.2 %all-to-all-start = ((f32[128,8,128]{2,0,1:T(8,128)}), f32[128,8,128]{2,0,1:T(8,128)S(1)}, u32[]{:S(2)}, u32[]{:S(2)}) async-start(f32[128,8,128]{2,0,1:T(8,128)} %fusion.16), calls=%async_computation | async-start | bytes 1048576 | tf_op jit(solution)/shard_map/all_to_all | solution.py:90
  61.4 83.4 %all-reduce.2.cloned.1.call-start = ((), (), s32[]{:S(2)}) async-start(), calls=%async_computation.2 | async-start | bytes 524288 | tf_op jit(solution)/shard_map/psum | solution.py:97
  61.7 0.7 copy-start.5
  62.4 0.7 copy-start.6
  75.8 1.8 %copy-start.7 = (f32[1,1024]{1,0:T(1,128)S(1)}, f32[1,1024]{1,0:T(1,128)}, u32[]{:S(2)}) copy-start(f32[1,1024]{1,0:T(1,128)} %param.14) | copy-start | bytes 12292
  144.9 2.4 %copy-start.1 = (f32[256,256]{1,0:T(8,128)S(1)}, f32[256,256]{1,0:T(8,128)}, u32[]{:S(2)}) copy-start(f32[256,256]{1,0:T(8,128)} %all-reduce.2.cloned.1.call-done) | copy-start | bytes 786436
Sparse Core Ops, SparseCore 0:
  93.6 51.2 all-reduce.1
where the time goes:
time: 176 us; the launch traced here: 175 us
  waiting for transfers between devices  86.7 us (49%)
  blocking collectives  24.1 us (14%)
  starting transfers between devices  18.5 us (11%)
  between operations  15.4 us (9%)
  local copies, waits for them, and re-layouts  12.7 us (7%)
  matrix products  11.3 us (6%)
  other arithmetic  6.67 us (4%)
    psum x1, waiting for transfers between devices, shards(): lax.psum((jnp.dot(weighted, deviation.T, precision=precise), jnp.dot(weig...  51.4 us
    ppermute x8, waiting for transfers between devices, extended(): before = lax.ppermute(last, axis, up)  16.8 us
    all_to_all x1, blocking collectives, shards(): lax.all_to_all(updated.reshape(-1, own_rows, cols_local), ('member', 'rol...  12.1 us
    psum x1, blocking collectives, shards(): lax.psum((jnp.dot(weighted, deviation.T, precision=precise), jnp.dot(weig...  12 us
    ppermute x8, waiting for transfers between devices, extended(): after = lax.ppermute(initial, axis, down)  10.5 us
    all_to_all x1, waiting for transfers between devices, shards(): lax.all_to_all(current, ('member', 'role'), split_axis=1, concat_axis=0,...  8.01 us
    ppermute x8, starting transfers between devices, extended(): before = lax.ppermute(last, axis, up)  7.91 us
    ppermute x8, starting transfers between devices, extended(): after = lax.ppermute(initial, axis, down)  6.87 us
  transfers between devices with their start and end apart: 18, of which 18 were waited for; matrix products, arithmetic and copies ran while one was open for 1% of the time, Pallas kernels for 0%

commit v1 on v0

--- a/solution.py
+++ b/solution.py
@@ -95,11 +95,14 @@
     deviation = observed - centre_obs
     weighted = deviation * jnp.where(usable, weights, jnp.float32(0.0))
     gram_sum, innovation = lax.psum(
-        (
-            jnp.dot(weighted, deviation.T, precision=precise),
-            jnp.dot(weighted, values - centre_obs, precision=precise),
+        lax.psum(
+            (
+                jnp.dot(weighted, deviation.T, precision=precise),
+                jnp.dot(weighted, values - centre_obs, precision=precise),
+            ),
+            "role",
         ),
-        ("member", "role"),
+        "member",
     )
     mixing = analysis_weights(gram_sum, innovation)
     flat_blocks = blocks.reshape(member_groups, role_groups, local_members, own_rows * cols_local)

time: 176 us -> 166 us (0.943)
  waiting for transfers between devices: 86.7 us -> 78.2 us
    psum x1, waiting for transfers between devices: 51.4 us -> 27.8 us  [shards(): lax.psum((jnp.dot(weighted, deviation.T, precision=precise), jnp.dot(weig...]
    psum x0 -> x1, waiting for transfers between devices: none -> 14.9 us  [shards(): lax.psum(lax.psum((jnp.dot(weighted, deviation.T, precision=precise), jnp...]
    psum x1, blocking collectives: 12 us -> 5.76 us  [shards(): lax.psum((jnp.dot(weighted, deviation.T, precision=precise), jnp.dot(weig...]
    psum x0 -> x1, blocking collectives: none -> 4.92 us  [shards(): lax.psum(lax.psum((jnp.dot(weighted, deviation.T, precision=precise), jnp...]
  transfers between devices with their start and end apart: 18 -> 19, of which waited for: 18 -> 19; matrix products, arithmetic and copies ran while one was open for 1% -> 2% of each run, Pallas kernels for 0% -> 0%
where the time goes in v1:
time: 166 us
  waiting for transfers between devices  78.2 us (47%)
  blocking collectives  22.9 us (14%)
  starting transfers between devices  18.5 us (11%)
  between operations  15.4 us (9%)
  local copies, waits for them, and re-layouts  12.7 us (8%)
  matrix products  11.3 us (7%)
  other arithmetic  6.68 us (4%)
    psum x1, waiting for transfers between devices, shards(): lax.psum((jnp.dot(weighted, deviation.T, precision=precise), jnp.dot(weig...  27.8 us
    ppermute x8, waiting for transfers between devices, extended(): before = lax.ppermute(last, axis, up)  16.8 us
    psum x1, waiting for transfers between devices, shards(): lax.psum(lax.psum((jnp.dot(weighted, deviation.T, precision=precise), jnp...  14.9 us
    all_to_all x1, blocking collectives, shards(): lax.all_to_all(updated.reshape(-1, own_rows, cols_local), ('member', 'rol...  12.3 us
    ppermute x8, waiting for transfers between devices, extended(): after = lax.ppermute(initial, axis, down)  10.5 us
    all_to_all x1, waiting for transfers between devices, shards(): lax.all_to_all(current, ('member', 'role'), split_axis=1, concat_axis=0,...  8.19 us
    ppermute x8, starting transfers between devices, extended(): before = lax.ppermute(last, axis, up)  7.91 us
    ppermute x8, starting transfers between devices, extended(): after = lax.ppermute(initial, axis, down)  6.87 us
  transfers between devices with their start and end apart: 19, of which 19 were waited for; matrix products, arithmetic and copies ran while one was open for 2% of the time, Pallas kernels for 0%

profile of v1, /device:TPU:0, one launch (start us, length us, event | category | flops | bytes accessed | tf_op | source)
XLA Modules:
  0.0 165.8 jit_solution(9116081184916549086)
XLA Ops:
  6.5 1.2 copy.67
  7.8 3.1 %collective-permute-start.1 = (f32[128,1,128]{2,0,1:T(8,128)S(1)}, f32[128,1,128]{2,0,1:T(8,128)S(1)}, u32[]{:S(2)}, u32[]{:S(2)}) collective-permute-start(f32[128,1,128]{2,0,1:T(8,128)S(1)} %get-tuple-element.20), channel_id=1, source_target_pairs={{0,4},{4,8},{8,12},{12,0},{1,5},{5,9},{9,13},{13,1},{2,6},{6,10},{... | collective-permute-start | bytes 196616 | tf_op jit(solution)/shard_map/ppermute | solution.py:18
  10.9 2.1 %collective-permute-start = (f32[128,1,128]{2,0,1:T(8,128)S(1)}, f32[128,1,128]{2,0,1:T(8,128)S(1)}, u32[]{:S(2)}, u32[]{:S(2)}) collective-permute-start(f32[128,1,128]{2,0,1:T(8,128)S(1)} %get-tuple-element.19), channel_id=1, source_target_pairs={{4,0},{8,4},{12,8},{0,12},{5,1},{9,5},{13,9},{1,13},{6,2},{10,6},{... | collective-permute-start | bytes 196616 | tf_op jit(solution)/shard_map/ppermute | solution.py:19
  13.0 2.3 %collective-permute-done.1 = f32[128,1,128]{2,0,1:T(8,128)S(1)} collective-permute-done((f32[128,1,128]{2,0,1:T(8,128)S(1)}, f32[128,1,128]{2,0,1:T(8,128)S(1)}, u32[]{:S(2)}, u32[]{:S(2)}) %collective-permute-start.1) | collective-permute-done | bytes 65568 | tf_op jit(solution)/shard_map/ppermute | solution.py:18
  15.3 0.5 collective-permute-done
  16.6 0.5 collective-permute-start.3
  17.1 0.6 collective-permute-done.2
  18.0 1.7 collective-permute-done.3
  19.9 0.5 fusion.46
  20.4 3.2 %collective-permute-start.4 = (f32[128,1,128]{2,0,1:T(8,128)S(1)}, f32[128,1,128]{2,0,1:T(8,128)S(1)}, u32[]{:S(2)}, u32[]{:S(2)}) collective-permute-start(f32[128,1,128]{2,0,1:T(8,128)S(1)} %get-tuple-element.18), channel_id=1, source_target_pairs={{4,0},{8,4},{12,8},{0,12},{5,1},{9,5},{13,9},{1,13},{6,2},{10,6},{... | collective-permute-start | bytes 196616 | tf_op jit(solution)/shard_map/ppermute | solution.py:19
  23.7 2.5 %collective-permute-done.4 = f32[128,1,128]{2,0,1:T(8,128)S(1)} collective-permute-done((f32[128,1,128]{2,0,1:T(8,128)S(1)}, f32[128,1,128]{2,0,1:T(8,128)S(1)}, u32[]{:S(2)}, u32[]{:S(2)}) %collective-permute-start.4) | collective-permute-done | bytes 65568 | tf_op jit(solution)/shard_map/ppermute | solution.py:19
  26.2 3.6 %collective-permute-done.5 = f32[128,1,128]{2,0,1:T(8,128)S(1)} collective-permute-done((f32[128,1,128]{2,0,1:T(8,128)S(1)}, f32[128,1,128]{2,0,1:T(8,128)S(1)}, u32[]{:S(2)}, u32[]{:S(2)}) %collective-permute-start.5) | collective-permute-done | bytes 65568 | tf_op jit(solution)/shard_map/ppermute | solution.py:18
  30.5 0.5 collective-permute-start.7
  31.1 0.6 collective-permute-done.6
  31.9 1.7 %collective-permute-done.7 = f32[128,10,1]{0,2,1:T(1,128)S(1)} collective-permute-done((f32[128,10,1]{0,2,1:T(1,128)S(1)}, f32[128,10,1]{0,2,1:T(1,128)S(1)}, u32[]{:S(2)}, u32[]{:S(2)}) %collective-permute-start.7) | collective-permute-done | bytes 5152 | tf_op jit(solution)/shard_map/ppermute | solution.py:18
  33.9 0.5 fusion.36
  34.4 0.8 collective-permute-start.8
  35.1 1.3 collective-permute-start.9
  36.5 2.2 %collective-permute-done.8 = f32[128,1,128]{2,0,1:T(8,128)S(1)} collective-permute-done((f32[128,1,128]{2,0,1:T(8,128)S(1)}, f32[128,1,128]{2,0,1:T(8,128)S(1)}, u32[]{:S(2)}, u32[]{:S(2)}) %collective-permute-start.8) | collective-permute-done | bytes 65568 | tf_op jit(solution)/shard_map/ppermute | solution.py:19
  38.7 2.5 %collective-permute-done.9 = f32[128,1,128]{2,0,1:T(8,128)S(1)} collective-permute-done((f32[128,1,128]{2,0,1:T(8,128)S(1)}, f32[128,1,128]{2,0,1:T(8,128)S(1)}, u32[]{:S(2)}, u32[]{:S(2)}) %collective-permute-start.9) | collective-permute-done | bytes 65568 | tf_op jit(solution)/shard_map/ppermute | solution.py:18
  42.0 0.5 collective-permute-start.11
  42.5 0.6 collective-permute-done.10
  43.4 1.7 %collective-permute-done.11 = f32[128,10,1]{0,2,1:T(1,128)S(1)} collective-permute-done((f32[128,10,1]{0,2,1:T(1,128)S(1)}, f32[128,10,1]{0,2,1:T(1,128)S(1)}, u32[]{:S(2)}, u32[]{:S(2)}) %collective-permute-start.11) | collective-permute-done | bytes 5152 | tf_op jit(solution)/shard_map/ppermute | solution.py:18
  45.3 0.5 fusion.26
  45.8 0.7 collective-permute-start.12
  46.5 1.4 collective-permute-start.13
  47.9 2.9 %collective-permute-done.12 = f32[128,1,128]{2,0,1:T(8,128)S(1)} collective-permute-done((f32[128,1,128]{2,0,1:T(8,128)S(1)}, f32[128,1,128]{2,0,1:T(8,128)S(1)}, u32[]{:S(2)}, u32[]{:S(2)}) %collective-permute-start.12) | collective-permute-done | bytes 65568 | tf_op jit(solution)/shard_map/ppermute | solution.py:19
  50.9 1.7 %collective-permute-done.13 = f32[128,1,128]{2,0,1:T(8,128)S(1)} collective-permute-done((f32[128,1,128]{2,0,1:T(8,128)S(1)}, f32[128,1,128]{2,0,1:T(8,128)S(1)}, u32[]{:S(2)}, u32[]{:S(2)}) %collective-permute-start.13) | collective-permute-done | bytes 65568 | tf_op jit(solution)/shard_map/ppermute | solution.py:18
  53.3 0.5 collective-permute-start.15
  53.8 0.6 collective-permute-done.14
  54.7 1.7 %collective-permute-done.15 = f32[128,10,1]{0,2,1:T(1,128)S(1)} collective-permute-done((f32[128,10,1]{0,2,1:T(1,128)S(1)}, f32[128,10,1]{0,2,1:T(1,128)S(1)}, u32[]{:S(2)}, u32[]{:S(2)}) %collective-permute-start.15) | collective-permute-done | bytes 5152 | tf_op jit(solution)/shard_map/ppermute | solution.py:18
  56.7 1.3 fusion.16
  57.9 3.5 %all-to-all-start = ((f32[128,8,128]{2,0,1:T(8,128)}), f32[128,8,128]{2,0,1:T(8,128)S(1)}, u32[]{:S(2)}, u32[]{:S(2)}) async-start(f32[128,8,128]{2,0,1:T(8,128)} %fusion.16), calls=%async_computation | async-start | bytes 1048576 | tf_op jit(solution)/shard_map/all_to_all | solution.py:90
  62.3 0.6 copy-done.6
  62.9 8.2 %all-to-all-done = f32[128,8,128]{2,0,1:T(8,128)S(1)} async-done(((f32[128,8,128]{2,0,1:T(8,128)}), f32[128,8,128]{2,0,1:T(8,128)S(1)}, u32[]{:S(2)}, u32[]{:S(2)}) %all-to-all-start) | async-done | bytes 524320 | tf_op jit(solution)/shard_map/all_to_all | solution.py:90
  71.4 4.5 %gather_fusion = f32[1024,2,128]{2,1,0:T(2,128)S(1)} fusion(f32[2,4,128,1,128]{2,0,4,3,1:T(2,128)S(1)} %copy.82, s32[1024]{0:T(1024)S(1)} %bitcast.100), kind=kCustom, calls=%fused_computation | custom fusion | bytes 2109440 | tf_op jit(solution)/shard_map/gather | solution.py:92
  75.8 1.8 %reduce_sum.34 = f32[1024]{0:T(1024)S(1)} reduce(f32[1024,2,128]{2,1,0:T(2,128)S(1)} %gather_fusion, f32[]{:T(128)} %constant.90.clone.1), dimensions={1,2}, to_apply=%region_0.1 | reduce | flops 261120 | bytes 1052676 | tf_op jit(solution)/shard_map/reduce_sum | solution.py:94
  77.7 3.0 %fusion = f32[256,256]{1,0:T(8,128)} fusion(f32[128,8,2,128]{3,2,1,0:T(2,128)S(1)} %bitcast.101, f32[1024]{0:T(1024)S(1)} %bitcast.108, f32[1024]{0:T(1024)S(1)} %get-tuple-element.22), kind=kOutput, calls=%fused_computation.2 | convolution fusion | flops 806092800 | bytes 1318912 | tf_op jit(solution)/shard_map/dot_general | solution.py:100
  80.9 0.8 fusion.9
  81.7 27.8 %all-reduce.3.cloned.1.call-done = f32[256,256]{1,0:T(8,128)} async-done(((f32[256,256]{1,0:T(8,128)}), f32[256,256]{1,0:T(8,128)}) %all-reduce.3.cloned.1.call-update) | async-done | bytes 262160 | tf_op jit(solution)/shard_map/psum | solution.py:98
  109.5 5.8 %psum.30 = f32[256]{0:T(256)S(1)} all-reduce(f32[256]{0:T(256)S(1)} %bitcast.113), channel_id=1, replica_groups=mesh['member'=2,'domain'=4,'role'=4] {'role'}, use_global_device_ids=true, to_apply=%region_4.5 | all-reduce | flops 256 | bytes 2048 | tf_op jit(solution)/shard_map/psum | solution.py:98
  115.3 4.9 %psum.31 = f32[256]{0:T(256)S(1)} all-reduce(f32[256]{0:T(256)S(1)} %psum.30), channel_id=1, replica_groups=mesh['member'=2,'domain'=4,'role'=4] {'member'}, use_global_device_ids=true, to_apply=%region_5.6 | all-reduce | flops 256 | bytes 2048 | tf_op jit(solution)/shard_map/psum | solution.py:97
  120.2 14.9 %all-reduce.5.cloned.1.call-done = f32[256,256]{1,0:T(8,128)} async-done(((f32[256,256]{1,0:T(8,128)}), f32[256,256]{1,0:T(8,128)}) %all-reduce.5.cloned.1.call-update) | async-done | bytes 262160 | tf_op jit(solution)/shard_map/psum | solution.py:97
  135.1 1.7 %multiply_reduce_fusion = f32[]{:T(128)} fusion(f32[256,256]{1,0:T(8,128)} %all-reduce.5.cloned.1.call-done), kind=kLoop, calls=%fused_computation.102 | loop fusion | flops 327679 | bytes 262148 | tf_op jit(solution)/shard_map/reduce_sum | solution.py:27
  138.1 0.4 fusion.59
  144.9 0.6 fusion.2
  145.6 12.3 %all_to_all.33 = f32[1024,1,128]{2,1,0:T(1,128)S(1)} all-to-all(f32[1024,1,128]{2,1,0:T(1,128)S(1)} %bitcast.105), channel_id=1, replica_groups=mesh['member'=2,'domain'=4,'role'=4] {'member','role'}, dimensions={0} | all-to-all | bytes 1048576 | tf_op jit(solution)/shard_map/all_to_all | solution.py:114
  157.8 1.1 copy.86
  (82 shorter events, 12.7 us)
Async XLA Ops:
  6.5 8.7 %copy-start = (f32[128,8,128]{2,1,0:T(8,128)S(1)}, f32[128,8,128]{2,1,0:T(8,128)}, u32[]{:S(2)}) copy-start(f32[128,8,128]{2,1,0:T(8,128)} %param.8) | copy-start | bytes 1572868
  7.8 7.5 %collective-permute-start.1 = (f32[128,1,128]{2,0,1:T(8,128)S(1)}, f32[128,1,128]{2,0,1:T(8,128)S(1)}, u32[]{:S(2)}, u32[]{:S(2)}) collective-permute-start(f32[128,1,128]{2,0,1:T(8,128)S(1)} %get-tuple-element.20), channel_id=1, source_target_pairs={{0,4},{4,8},{8,12},{12,0},{1,5},{5,9},{9,13},{13,1},{2,6},{6,10},{... | collective-permute-start | bytes 196616 | tf_op jit(solution)/shard_map/ppermute | solution.py:18
  10.9 5.0 %collective-permute-start = (f32[128,1,128]{2,0,1:T(8,128)S(1)}, f32[128,1,128]{2,0,1:T(8,128)S(1)}, u32[]{:S(2)}, u32[]{:S(2)}) collective-permute-start(f32[128,1,128]{2,0,1:T(8,128)S(1)} %get-tuple-element.19), channel_id=1, source_target_pairs={{4,0},{8,4},{12,8},{0,12},{5,1},{9,5},{13,9},{1,13},{6,2},{10,6},{... | collective-permute-start | bytes 196616 | tf_op jit(solution)/shard_map/ppermute | solution.py:19
  16.3 1.4 collective-permute-start.2
  16.6 3.1 %collective-permute-start.3 = (f32[128,10,1]{0,2,1:T(1,128)S(1)}, f32[128,10,1]{0,2,1:T(1,128)S(1)}, u32[]{:S(2)}, u32[]{:S(2)}) collective-permute-start(f32[128,10,1]{0,2,1:T(1,128)S(1)} %copy.64), channel_id=1, source_target_pairs={{0,1},{1,2},{2,3},{3,0},{4,5},{5,6},{6,7},{7,4},{8,9},{9,10},{10,1... | collective-permute-start | bytes 15368 | tf_op jit(solution)/shard_map/ppermute | solution.py:18
  17.9 2.0 %copy-start.2 = (f32[8,128]{1,0:T(8,128)S(1)}, f32[8,128]{1,0:T(8,128)}, u32[]{:S(2)}) copy-start(f32[8,128]{1,0:T(8,128)} %param.11) | copy-start | bytes 12292
  18.0 2.0 %copy-start.3 = (f32[8,128]{1,0:T(8,128)S(1)}, f32[8,128]{1,0:T(8,128)}, u32[]{:S(2)}) copy-start(f32[8,128]{1,0:T(8,128)} %param.10) | copy-start | bytes 12292
  18.0 2.0 %copy-start.4 = (f32[8,128]{1,0:T(8,128)S(1)}, f32[8,128]{1,0:T(8,128)}, u32[]{:S(2)}) copy-start(f32[8,128]{1,0:T(8,128)} %param.9) | copy-start | bytes 12292
  20.4 5.7 %collective-permute-start.4 = (f32[128,1,128]{2,0,1:T(8,128)S(1)}, f32[128,1,128]{2,0,1:T(8,128)S(1)}, u32[]{:S(2)}, u32[]{:S(2)}) collective-permute-start(f32[128,1,128]{2,0,1:T(8,128)S(1)} %get-tuple-element.18), channel_id=1, source_target_pairs={{4,0},{8,4},{12,8},{0,12},{5,1},{9,5},{13,9},{1,13},{6,2},{10,6},{... | collective-permute-start | bytes 196616 | tf_op jit(solution)/shard_map/ppermute | solution.py:19
  23.7 6.1 %collective-permute-start.5 = (f32[128,1,128]{2,0,1:T(8,128)S(1)}, f32[128,1,128]{2,0,1:T(8,128)S(1)}, u32[]{:S(2)}, u32[]{:S(2)}) collective-permute-start(f32[128,1,128]{2,0,1:T(8,128)S(1)} %get-tuple-element.17), channel_id=1, source_target_pairs={{0,4},{4,8},{8,12},{12,0},{1,5},{5,9},{9,13},{13,1},{2,6},{6,10},{... | collective-permute-start | bytes 196616 | tf_op jit(solution)/shard_map/ppermute | solution.py:18
  30.3 1.4 collective-permute-start.6
  30.5 3.1 %collective-permute-start.7 = (f32[128,10,1]{0,2,1:T(1,128)S(1)}, f32[128,10,1]{0,2,1:T(1,128)S(1)}, u32[]{:S(2)}, u32[]{:S(2)}) collective-permute-start(f32[128,10,1]{0,2,1:T(1,128)S(1)} %copy.72), channel_id=1, source_target_pairs={{0,1},{1,2},{2,3},{3,0},{4,5},{5,6},{6,7},{7,4},{8,9},{9,10},{10,1... | collective-permute-start | bytes 15368 | tf_op jit(solution)/shard_map/ppermute | solution.py:18
  34.4 4.3 %collective-permute-start.8 = (f32[128,1,128]{2,0,1:T(8,128)S(1)}, f32[128,1,128]{2,0,1:T(8,128)S(1)}, u32[]{:S(2)}, u32[]{:S(2)}) collective-permute-start(f32[128,1,128]{2,0,1:T(8,128)S(1)} %get-tuple-element.16), channel_id=1, source_target_pairs={{4,0},{8,4},{12,8},{0,12},{5,1},{9,5},{13,9},{1,13},{6,2},{10,6},{... | collective-permute-start | bytes 196616 | tf_op jit(solution)/shard_map/ppermute | solution.py:19
  35.1 6.1 %collective-permute-start.9 = (f32[128,1,128]{2,0,1:T(8,128)S(1)}, f32[128,1,128]{2,0,1:T(8,128)S(1)}, u32[]{:S(2)}, u32[]{:S(2)}) collective-permute-start(f32[128,1,128]{2,0,1:T(8,128)S(1)} %get-tuple-element.15), channel_id=1, source_target_pairs={{0,4},{4,8},{8,12},{12,0},{1,5},{5,9},{9,13},{13,1},{2,6},{6,10},{... | collective-permute-start | bytes 196616 | tf_op jit(solution)/shard_map/ppermute | solution.py:18
  41.7 1.4 collective-permute-start.10
  42.0 3.1 %collective-permute-start.11 = (f32[128,10,1]{0,2,1:T(1,128)S(1)}, f32[128,10,1]{0,2,1:T(1,128)S(1)}, u32[]{:S(2)}, u32[]{:S(2)}) collective-permute-start(f32[128,10,1]{0,2,1:T(1,128)S(1)} %copy.76), channel_id=1, source_target_pairs={{0,1},{1,2},{2,3},{3,0},{4,5},{5,6},{6,7},{7,4},{8,9},{9,10},{10,1... | collective-permute-start | bytes 15368 | tf_op jit(solution)/shard_map/ppermute | solution.py:18
  45.8 5.0 %collective-permute-start.12 = (f32[128,1,128]{2,0,1:T(8,128)S(1)}, f32[128,1,128]{2,0,1:T(8,128)S(1)}, u32[]{:S(2)}, u32[]{:S(2)}) collective-permute-start(f32[128,1,128]{2,0,1:T(8,128)S(1)} %get-tuple-element.14), channel_id=1, source_target_pairs={{4,0},{8,4},{12,8},{0,12},{5,1},{9,5},{13,9},{1,13},{6,2},{10,6},{... | collective-permute-start | bytes 196616 | tf_op jit(solution)/shard_map/ppermute | solution.py:19
  46.5 6.1 %collective-permute-start.13 = (f32[128,1,128]{2,0,1:T(8,128)S(1)}, f32[128,1,128]{2,0,1:T(8,128)S(1)}, u32[]{:S(2)}, u32[]{:S(2)}) collective-permute-start(f32[128,1,128]{2,0,1:T(8,128)S(1)} %get-tuple-element.13), channel_id=1, source_target_pairs={{0,4},{4,8},{8,12},{12,0},{1,5},{5,9},{9,13},{13,1},{2,6},{6,10},{... | collective-permute-start | bytes 196616 | tf_op jit(solution)/shard_map/ppermute | solution.py:18
  53.1 1.4 collective-permute-start.14
  53.3 3.1 %collective-permute-start.15 = (f32[128,10,1]{0,2,1:T(1,128)S(1)}, f32[128,10,1]{0,2,1:T(1,128)S(1)}, u32[]{:S(2)}, u32[]{:S(2)}) collective-permute-start(f32[128,10,1]{0,2,1:T(1,128)S(1)} %copy.80), channel_id=1, source_target_pairs={{0,1},{1,2},{2,3},{3,0},{4,5},{5,6},{6,7},{7,4},{8,9},{9,10},{10,1... | collective-permute-start | bytes 15368 | tf_op jit(solution)/shard_map/ppermute | solution.py:18
  57.9 13.2 %all-to-all-start = ((f32[128,8,128]{2,0,1:T(8,128)}), f32[128,8,128]{2,0,1:T(8,128)S(1)}, u32[]{:S(2)}, u32[]{:S(2)}) async-start(f32[128,8,128]{2,0,1:T(8,128)} %fusion.16), calls=%async_computation | async-start | bytes 1048576 | tf_op jit(solution)/shard_map/all_to_all | solution.py:90
  61.4 48.0 %all-reduce.3.cloned.1.call-start = ((), (), s32[]{:S(2)}) async-start(), calls=%async_computation.2 | async-start | bytes 524288 | tf_op jit(solution)/shard_map/psum | solution.py:98
  61.5 0.7 copy-start.5
  62.2 0.7 copy-start.6
  75.8 1.8 %copy-start.7 = (f32[1,1024]{1,0:T(1,128)S(1)}, f32[1,1024]{1,0:T(1,128)}, u32[]{:S(2)}) copy-start(f32[1,1024]{1,0:T(1,128)} %param.14) | copy-start | bytes 12292
  80.7 54.4 %all-reduce.5.cloned.1.call-start = ((), (), s32[]{:S(2)}) async-start(), calls=%async_computation.3 | async-start | bytes 524288 | tf_op jit(solution)/shard_map/psum | solution.py:97
  135.1 2.4 %copy-start.1 = (f32[256,256]{1,0:T(8,128)S(1)}, f32[256,256]{1,0:T(8,128)}, u32[]{:S(2)}) copy-start(f32[256,256]{1,0:T(8,128)} %all-reduce.5.cloned.1.call-done) | copy-start | bytes 786436
Sparse Core Ops, SparseCore 0:
  80.8 28.5 all-reduce.2
  111.7 23.3 all-reduce.4
